TPU v7x, 32 devices: a whole 2x2x4 slice. The times are simulated.
32 devices in a mesh: slab: 8 (over y, x, core), blk: 4 (over z).
Axes of the slice: x: 2, y: 2, z: 4, core: 2. Of those that a mesh axis runs over, the one named last changes fastest.
Arguments:
- start_block: float32 [128, 64, 8, 128], P('blk', 'slab'), as said below
- locked_modes: float32 [384, 64, 8, 128], P('blk', 'slab'), as said below
- material: int32 [64, 8, 128], P('slab'), may hold values 0 or 1
- support: int32 [8, 128], replicated, may hold values 0 or 1
Outputs:
- basis: float32 [128, 64, 8, 128], P('blk', 'slab')
Inputs may be any that keep to these rules, and one draw needn't show every extreme that they name: `start_block`: A block of random vectors with large parts along the locked modes. `locked_modes`: each locked mode (one row) has about unit norm over all voxels.
All inputs are finite; a program needn't handle non-finite values. No bound on the sum of `material` on one device may be relied on, other than what follows from the above.
Results may differ from a plain program's by a relative error of at most 0.00014.
Values sent between devices are 32-bit elements; how exact they have to be, the bound alone decides.
No kernel may reach another device: no remote copies, remote signals or barrier semaphores. Data moves between devices by JAX's collectives and lax.ppermute only.
A program may use at most 64 MiB of HBM per device.

v0:
```python
import jax
import jax.numpy as jnp
from jax import lax
from jax.sharding import PartitionSpec as P

DEGREE = 8
THETA_LOAD = 0.1
VOID_ROOT = 0.31622776601683794
FILTER_CENTRE = 9.0
FILTER_HALF = 7.5


def padded_2(cells, sides, width):
    for axis, dim in sides:
        count = lax.axis_size(axis)
        ends = count - 1
        head = lax.slice_in_dim(cells, 0, width, axis=dim)
        tail = lax.slice_in_dim(cells, cells.shape[dim] - width, cells.shape[dim], axis=dim)
        cells = jnp.concatenate(
            [
                lax.ppermute(tail, axis, [(i, (i + 1) % count) for i in range(ends)]),
                cells,
                lax.ppermute(head, axis, [((i + 1) % count, i) for i in range(ends)]),
            ],
            axis=dim,
        )
    return cells


def blurred(padded):
    along_z = 0.5 * padded[:, :-2] + padded[:, 1:-1] + 0.5 * padded[:, 2:]
    along_y = 0.5 * along_z[:, :, :-2] + along_z[:, :, 1:-1] + 0.5 * along_z[:, :, 2:]
    along_x = 0.5 * along_y[..., :-2] + along_y[..., 1:-1] + 0.5 * along_y[..., 2:]
    return 2.0 * along_x


def operate(field, free_cells, root_stiff):
    kept_field = free_cells * field
    weighted = root_stiff * kept_field
    extended = padded_2(weighted, (("slab", 1),), 1)
    padded = jnp.pad(extended, ((0, 0), (0, 0), (1, 1), (1, 1)))
    smooth = blurred(padded)
    neighbours = padded[:, 2:, 1:-1, 1:-1] + padded[:, :-2, 1:-1, 1:-1]
    elastic = root_stiff * (16.0 * weighted - smooth)
    geometric = THETA_LOAD * root_stiff * (2.0 * weighted - neighbours)
    return free_cells * (elastic - geometric + 0.5 * kept_field) + (1.0 - free_cells) * field


def lower_inverse(gram):
    lower_factor = jnp.linalg.cholesky(gram)
    identity = jnp.eye(gram.shape[0], dtype=jnp.float32)
    return jax.scipy.linalg.solve_triangular(lower_factor, identity, lower=True)


def per_device(start_block, locked_modes, material, support):
    depth = material.shape[0]
    root_stiff = jnp.where(material == 1, 1.0, VOID_ROOT).astype(jnp.float32)
    layer = lax.axis_index("slab") * depth + lax.broadcasted_iota(jnp.int32, material.shape, 0)
    clamped = jnp.where(layer == 0, support[None, :, :], 0)
    free_cells = (1 - clamped).astype(jnp.float32)
    previous = start_block
    current = (
        operate(start_block, free_cells, root_stiff) - FILTER_CENTRE * start_block
    ) / FILTER_HALF
    for order_index in range(DEGREE - 1):
        following = (
            2.0 * (operate(current, free_cells, root_stiff) - FILTER_CENTRE * current) / FILTER_HALF
            - previous
        )
        previous = current
        current = following
    own_count = start_block.shape[0]
    cells = depth * start_block.shape[2] * start_block.shape[3]
    total_cells = cells * lax.axis_size("slab")
    flat = current.reshape(own_count, cells)
    modes_flat = locked_modes.reshape(locked_modes.shape[0], cells)
    gathered = lax.all_gather(flat, "blk", axis=0, tiled=True)
    correlations = lax.psum(
        jnp.dot(
            modes_flat,
            gathered.T,
            precision=lax.Precision.HIGHEST,
            preferred_element_type=jnp.float32,
        ),
        "slab",
    )
    own_deflated = flat - lax.psum_scatter(
        jnp.dot(
            correlations.T,
            modes_flat,
            precision=lax.Precision.HIGHEST,
            preferred_element_type=jnp.float32,
        ),
        "blk",
        scatter_dimension=0,
        tiled=True,
    )
    deflated = lax.all_gather(own_deflated, "blk", axis=0, tiled=True)
    gram = lax.psum(
        jnp.dot(
            deflated,
            deflated.T,
            precision=lax.Precision.HIGHEST,
            preferred_element_type=jnp.float32,
        ),
        "slab",
    )
    inverse = lower_inverse(gram)
    own_rows = lax.dynamic_slice_in_dim(inverse, lax.axis_index("blk") * own_count, own_count, 0)
    basis = jnp.sqrt(jnp.float32(total_cells)) * jnp.dot(
        own_rows, deflated, precision=lax.Precision.HIGHEST, preferred_element_type=jnp.float32
    )
    return basis.reshape(start_block.shape)


def solution(mesh):
    in_specs = (
        P("blk", "slab", None, None),
        P("blk", "slab", None, None),
        P("slab", None, None),
        P(),
    )
    out_specs = P("blk", "slab", None, None)
    return jax.shard_map(
        per_device, mesh=mesh, in_specs=in_specs, out_specs=out_specs, check_vma=False
    )
```

profile of v0, /device:TPU:0, one launch (start us, length us, event | category | flops | bytes accessed | tf_op | source)
XLA Modules:
  0.0 502.9 jit_solution(1023885015626496293)
XLA Ops:
  10.8 3.0 collective-permute-start
  14.8 2.2 select_maximum_fusion.14
  21.6 6.1 %collective-permute-start.2 = (f32[32,1,8,128]{3,2,1,0:T(8,128)S(1)}, f32[32,1,8,128]{3,2,1,0:T(8,128)S(1)}, u32[]{:S(2)}, u32[]{:S(2)}) collective-permute-start(f32[32,1,8,128]{3,2,1,0:T(8,128)S(1)} %get-tuple-element.32), channel_id=1, source_target_pairs={{0,4},{4,8},{8,12},{12,16},{16,20},{20,24},{24,28},{1,5},{5,9},{9,... | collective-permute-start | bytes 393224 | tf_op jit(solution)/shard_map/ppermute | solution.py:21
  28.7 2.2 select_maximum_fusion.12
  34.9 6.1 %collective-permute-start.4 = (f32[32,1,8,128]{3,2,1,0:T(8,128)S(1)}, f32[32,1,8,128]{3,2,1,0:T(8,128)S(1)}, u32[]{:S(2)}, u32[]{:S(2)}) collective-permute-start(f32[32,1,8,128]{3,2,1,0:T(8,128)S(1)} %get-tuple-element.30), channel_id=1, source_target_pairs={{0,4},{4,8},{8,12},{12,16},{16,20},{20,24},{24,28},{1,5},{5,9},{9,... | collective-permute-start | bytes 393224 | tf_op jit(solution)/shard_map/ppermute | solution.py:21
  41.8 2.2 select_maximum_fusion.10
  48.1 5.9 %collective-permute-start.6 = (f32[32,1,8,128]{3,2,1,0:T(8,128)S(1)}, f32[32,1,8,128]{3,2,1,0:T(8,128)S(1)}, u32[]{:S(2)}, u32[]{:S(2)}) collective-permute-start(f32[32,1,8,128]{3,2,1,0:T(8,128)S(1)} %get-tuple-element.28), channel_id=1, source_target_pairs={{0,4},{4,8},{8,12},{12,16},{16,20},{20,24},{24,28},{1,5},{5,9},{9,... | collective-permute-start | bytes 393224 | tf_op jit(solution)/shard_map/ppermute | solution.py:21
  55.0 2.2 select_maximum_fusion.8
  61.3 5.9 %collective-permute-start.8 = (f32[32,1,8,128]{3,2,1,0:T(8,128)S(1)}, f32[32,1,8,128]{3,2,1,0:T(8,128)S(1)}, u32[]{:S(2)}, u32[]{:S(2)}) collective-permute-start(f32[32,1,8,128]{3,2,1,0:T(8,128)S(1)} %get-tuple-element.26), channel_id=1, source_target_pairs={{0,4},{4,8},{8,12},{12,16},{16,20},{20,24},{24,28},{1,5},{5,9},{9,... | collective-permute-start | bytes 393224 | tf_op jit(solution)/shard_map/ppermute | solution.py:21
  74.4 6.2 %collective-permute-start.10 = (f32[32,1,8,128]{3,2,1,0:T(8,128)S(1)}, f32[32,1,8,128]{3,2,1,0:T(8,128)S(1)}, u32[]{:S(2)}, u32[]{:S(2)}) collective-permute-start(f32[32,1,8,128]{3,2,1,0:T(8,128)S(1)} %get-tuple-element.24), channel_id=1, source_target_pairs={{0,4},{4,8},{8,12},{12,16},{16,20},{20,24},{24,28},{1,5},{5,9},{9,... | collective-permute-start | bytes 393224 | tf_op jit(solution)/shard_map/ppermute | solution.py:21
  87.6 5.9 %collective-permute-start.12 = (f32[32,1,8,128]{3,2,1,0:T(8,128)S(1)}, f32[32,1,8,128]{3,2,1,0:T(8,128)S(1)}, u32[]{:S(2)}, u32[]{:S(2)}) collective-permute-start(f32[32,1,8,128]{3,2,1,0:T(8,128)S(1)} %get-tuple-element.22), channel_id=1, source_target_pairs={{0,4},{4,8},{8,12},{12,16},{16,20},{20,24},{24,28},{1,5},{5,9},{9,... | collective-permute-start | bytes 393224 | tf_op jit(solution)/shard_map/ppermute | solution.py:21
  100.8 6.6 %collective-permute-start.14 = (f32[32,1,8,128]{3,2,1,0:T(8,128)S(1)}, f32[32,1,8,128]{3,2,1,0:T(8,128)S(1)}, u32[]{:S(2)}, u32[]{:S(2)}) collective-permute-start(f32[32,1,8,128]{3,2,1,0:T(8,128)S(1)} %get-tuple-element.20), channel_id=1, source_target_pairs={{0,4},{4,8},{8,12},{12,16},{16,20},{20,24},{24,28},{1,5},{5,9},{9,... | collective-permute-start | bytes 393224 | tf_op jit(solution)/shard_map/ppermute | solution.py:21
  115.5 93.3 %all-gather.3.cloned.1.call-done = f32[128,8192]{1,0:T(8,128)} async-done(((f32[32,8192]{1,0:T(8,128)}), f32[128,8192]{1,0:T(8,128)}) %all-gather.3.cloned.1.call-update) | async-done | bytes 4194320 | tf_op jit(solution)/shard_map/all_gather | solution.py:77
  208.7 7.6 %fusion.26 = f32[96,128]{0,1:T(8,128)S(1)} fusion(f32[128,8192]{1,0:T(8,128)} %all-gather.3.cloned.1.call-done, f32[12,8,64,128]{3,2,1,0:T(8,128)S(1)} %bitcast.36), kind=kOutput, calls=%fused_computation.95 | convolution fusion | flops 1207959552 | bytes 7389184 | tf_op jit(solution)/shard_map/dot_general | solution.py:79
  216.4 24.3 %psum.14 = f32[96,128]{0,1:T(8,128)S(1)} all-reduce(f32[96,128]{0,1:T(8,128)S(1)} %fusion.26), channel_id=1, replica_groups=mesh['slab'=8,'blk'=4] {'slab'}, use_global_device_ids=true, to_apply=%region_0.1 | all-reduce | flops 12288 | bytes 98304 | tf_op jit(solution)/shard_map/psum | solution.py:78
  240.7 7.9 %fusion.11 = f32[128,8192]{1,0:T(8,128)} fusion(f32[96,128]{0,1:T(8,128)S(1)} %psum.14, f32[12,8,64,128]{3,2,1,0:T(8,128)S(1)} %bitcast.37), kind=kOutput, calls=%fused_computation.56 | convolution fusion | flops 1207959552 | bytes 7389184 | tf_op jit(solution)/shard_map/dot_general | solution.py:88
  248.6 73.7 %reduce-scatter.2.cloned.1.call-done = f32[32,8192]{1,0:T(8,128)} async-done(((f32[128,8192]{1,0:T(8,128)}), f32[32,8192]{1,0:T(8,128)}) %reduce-scatter.2.cloned.1.call-update) | async-done | bytes 1048592 | tf_op jit(solution)/shard_map/reduce_scatter | solution.py:87
  322.4 2.8 fusion.147
  325.4 81.2 %all-gather.5.cloned.1.call-done = f32[128,8192]{1,0:T(8,128)} async-done(((f32[32,8192]{1,0:T(8,128)}), f32[128,8192]{1,0:T(8,128)}) %all-gather.5.cloned.1.call-update) | async-done | bytes 4194320 | tf_op jit(solution)/shard_map/all_gather | solution.py:98
  406.6 7.6 %fusion.163 = f32[128,128]{0,1:T(8,128)} fusion(f32[128,8192]{1,0:T(8,128)} %all-gather.5.cloned.1.call-done), kind=kOutput, calls=%fused_computation.283 | convolution fusion | flops 1610612736 | bytes 4259840 | tf_op jit(solution)/shard_map/dot_general | solution.py:100
  414.3 51.8 %all-reduce.10.cloned.1.call-done = f32[128,128]{0,1:T(8,128)} async-done(((f32[128,128]{0,1:T(8,128)}), f32[128,128]{0,1:T(8,128)}) %all-reduce.10.cloned.1.call-update) | async-done | bytes 65552 | tf_op jit(solution)/shard_map/psum | solution.py:99
  467.9 11.7 %cholesky.17 = f32[128,128]{1,0:T(8,128)S(1)} custom-call(f32[128,128]{1,0:T(8,128)S(1)} %fusion.142), custom_call_target="Cholesky" | custom-call | tf_op jit(solution)/shard_map/jit(cholesky)/cholesky | solution.py:50
  480.9 9.8 %custom-call.7 = f32[1,128,128]{1,2,0:T(8,128)S(1)} custom-call(f32[1,128,128]{2,1,0:T(8,128)S(1)} %fusion.139), custom_call_target="InvertDiagBlocksLowerTriangular" | custom-call | tf_op jit(solution)/shard_map/jit(_solve_triangular)/triangular_solve | solution.py:52
  491.0 4.0 fusion.25
  (89 shorter events, 58.4 us)
Async XLA Ops:
  6.5 202.2 %all-gather.3.cloned.1.call-start = ((), (), s32[]{:S(2)}) async-start(), calls=%async_computation.1 | async-start | bytes 5242880 | tf_op jit(solution)/shard_map/all_gather | solution.py:77
  9.5 5.1 %collective-permute-start.1 = (f32[32,1,8,128]{3,2,1,0:T(8,128)S(1)}, f32[32,1,8,128]{3,2,1,0:T(8,128)S(1)}, u32[]{:S(2)}, u32[]{:S(2)}) collective-permute-start(f32[32,1,8,128]{3,2,1,0:T(8,128)S(1)} %get-tuple-element.33), channel_id=1, source_target_pairs={{4,0},{8,4},{12,8},{16,12},{20,16},{24,20},{28,24},{5,1},{9,5},{13... | collective-permute-start | bytes 393224 | tf_op jit(solution)/shard_map/ppermute | solution.py:23
  10.8 4.0 collective-permute-start
  18.0 1.2 copy-start.1
  20.3 7.4 %collective-permute-start.3 = (f32[32,1,8,128]{3,2,1,0:T(8,128)S(1)}, f32[32,1,8,128]{3,2,1,0:T(8,128)S(1)}, u32[]{:S(2)}, u32[]{:S(2)}) collective-permute-start(f32[32,1,8,128]{3,2,1,0:T(8,128)S(1)} %get-tuple-element.31), channel_id=1, source_target_pairs={{4,0},{8,4},{12,8},{16,12},{20,16},{24,20},{28,24},{5,1},{9,5},{13... | collective-permute-start | bytes 393224 | tf_op jit(solution)/shard_map/ppermute | solution.py:23
  21.6 7.1 %collective-permute-start.2 = (f32[32,1,8,128]{3,2,1,0:T(8,128)S(1)}, f32[32,1,8,128]{3,2,1,0:T(8,128)S(1)}, u32[]{:S(2)}, u32[]{:S(2)}) collective-permute-start(f32[32,1,8,128]{3,2,1,0:T(8,128)S(1)} %get-tuple-element.32), channel_id=1, source_target_pairs={{0,4},{4,8},{8,12},{12,16},{16,20},{20,24},{24,28},{1,5},{5,9},{9,... | collective-permute-start | bytes 393224 | tf_op jit(solution)/shard_map/ppermute | solution.py:21
  33.6 7.4 %collective-permute-start.5 = (f32[32,1,8,128]{3,2,1,0:T(8,128)S(1)}, f32[32,1,8,128]{3,2,1,0:T(8,128)S(1)}, u32[]{:S(2)}, u32[]{:S(2)}) collective-permute-start(f32[32,1,8,128]{3,2,1,0:T(8,128)S(1)} %get-tuple-element.29), channel_id=1, source_target_pairs={{4,0},{8,4},{12,8},{16,12},{20,16},{24,20},{28,24},{5,1},{9,5},{13... | collective-permute-start | bytes 393224 | tf_op jit(solution)/shard_map/ppermute | solution.py:23
  34.9 6.9 %collective-permute-start.4 = (f32[32,1,8,128]{3,2,1,0:T(8,128)S(1)}, f32[32,1,8,128]{3,2,1,0:T(8,128)S(1)}, u32[]{:S(2)}, u32[]{:S(2)}) collective-permute-start(f32[32,1,8,128]{3,2,1,0:T(8,128)S(1)} %get-tuple-element.30), channel_id=1, source_target_pairs={{0,4},{4,8},{8,12},{12,16},{16,20},{20,24},{24,28},{1,5},{5,9},{9,... | collective-permute-start | bytes 393224 | tf_op jit(solution)/shard_map/ppermute | solution.py:21
  46.8 7.3 %collective-permute-start.7 = (f32[32,1,8,128]{3,2,1,0:T(8,128)S(1)}, f32[32,1,8,128]{3,2,1,0:T(8,128)S(1)}, u32[]{:S(2)}, u32[]{:S(2)}) collective-permute-start(f32[32,1,8,128]{3,2,1,0:T(8,128)S(1)} %get-tuple-element.27), channel_id=1, source_target_pairs={{4,0},{8,4},{12,8},{16,12},{20,16},{24,20},{28,24},{5,1},{9,5},{13... | collective-permute-start | bytes 393224 | tf_op jit(solution)/shard_map/ppermute | solution.py:23
  48.1 6.9 %collective-permute-start.6 = (f32[32,1,8,128]{3,2,1,0:T(8,128)S(1)}, f32[32,1,8,128]{3,2,1,0:T(8,128)S(1)}, u32[]{:S(2)}, u32[]{:S(2)}) collective-permute-start(f32[32,1,8,128]{3,2,1,0:T(8,128)S(1)} %get-tuple-element.28), channel_id=1, source_target_pairs={{0,4},{4,8},{8,12},{12,16},{16,20},{20,24},{24,28},{1,5},{5,9},{9,... | collective-permute-start | bytes 393224 | tf_op jit(solution)/shard_map/ppermute | solution.py:21
  60.0 7.3 %collective-permute-start.9 = (f32[32,1,8,128]{3,2,1,0:T(8,128)S(1)}, f32[32,1,8,128]{3,2,1,0:T(8,128)S(1)}, u32[]{:S(2)}, u32[]{:S(2)}) collective-permute-start(f32[32,1,8,128]{3,2,1,0:T(8,128)S(1)} %get-tuple-element.25), channel_id=1, source_target_pairs={{4,0},{8,4},{12,8},{16,12},{20,16},{24,20},{28,24},{5,1},{9,5},{13... | collective-permute-start | bytes 393224 | tf_op jit(solution)/shard_map/ppermute | solution.py:23
  61.3 6.9 %collective-permute-start.8 = (f32[32,1,8,128]{3,2,1,0:T(8,128)S(1)}, f32[32,1,8,128]{3,2,1,0:T(8,128)S(1)}, u32[]{:S(2)}, u32[]{:S(2)}) collective-permute-start(f32[32,1,8,128]{3,2,1,0:T(8,128)S(1)} %get-tuple-element.26), channel_id=1, source_target_pairs={{0,4},{4,8},{8,12},{12,16},{16,20},{20,24},{24,28},{1,5},{5,9},{9,... | collective-permute-start | bytes 393224 | tf_op jit(solution)/shard_map/ppermute | solution.py:21
  73.1 7.5 %collective-permute-start.11 = (f32[32,1,8,128]{3,2,1,0:T(8,128)S(1)}, f32[32,1,8,128]{3,2,1,0:T(8,128)S(1)}, u32[]{:S(2)}, u32[]{:S(2)}) collective-permute-start(f32[32,1,8,128]{3,2,1,0:T(8,128)S(1)} %get-tuple-element.23), channel_id=1, source_target_pairs={{4,0},{8,4},{12,8},{16,12},{20,16},{24,20},{28,24},{5,1},{9,5},{13... | collective-permute-start | bytes 393224 | tf_op jit(solution)/shard_map/ppermute | solution.py:23
  74.4 6.9 %collective-permute-start.10 = (f32[32,1,8,128]{3,2,1,0:T(8,128)S(1)}, f32[32,1,8,128]{3,2,1,0:T(8,128)S(1)}, u32[]{:S(2)}, u32[]{:S(2)}) collective-permute-start(f32[32,1,8,128]{3,2,1,0:T(8,128)S(1)} %get-tuple-element.24), channel_id=1, source_target_pairs={{0,4},{4,8},{8,12},{12,16},{16,20},{20,24},{24,28},{1,5},{5,9},{9,... | collective-permute-start | bytes 393224 | tf_op jit(solution)/shard_map/ppermute | solution.py:21
  86.3 7.3 %collective-permute-start.13 = (f32[32,1,8,128]{3,2,1,0:T(8,128)S(1)}, f32[32,1,8,128]{3,2,1,0:T(8,128)S(1)}, u32[]{:S(2)}, u32[]{:S(2)}) collective-permute-start(f32[32,1,8,128]{3,2,1,0:T(8,128)S(1)} %get-tuple-element.21), channel_id=1, source_target_pairs={{4,0},{8,4},{12,8},{16,12},{20,16},{24,20},{28,24},{5,1},{9,5},{13... | collective-permute-start | bytes 393224 | tf_op jit(solution)/shard_map/ppermute | solution.py:23
  87.6 6.9 %collective-permute-start.12 = (f32[32,1,8,128]{3,2,1,0:T(8,128)S(1)}, f32[32,1,8,128]{3,2,1,0:T(8,128)S(1)}, u32[]{:S(2)}, u32[]{:S(2)}) collective-permute-start(f32[32,1,8,128]{3,2,1,0:T(8,128)S(1)} %get-tuple-element.22), channel_id=1, source_target_pairs={{0,4},{4,8},{8,12},{12,16},{16,20},{20,24},{24,28},{1,5},{5,9},{9,... | collective-permute-start | bytes 393224 | tf_op jit(solution)/shard_map/ppermute | solution.py:21
  99.5 7.9 %collective-permute-start.15 = (f32[32,1,8,128]{3,2,1,0:T(8,128)S(1)}, f32[32,1,8,128]{3,2,1,0:T(8,128)S(1)}, u32[]{:S(2)}, u32[]{:S(2)}) collective-permute-start(f32[32,1,8,128]{3,2,1,0:T(8,128)S(1)} %get-tuple-element.19), channel_id=1, source_target_pairs={{4,0},{8,4},{12,8},{16,12},{20,16},{24,20},{28,24},{5,1},{9,5},{13... | collective-permute-start | bytes 393224 | tf_op jit(solution)/shard_map/ppermute | solution.py:23
  100.8 7.1 %collective-permute-start.14 = (f32[32,1,8,128]{3,2,1,0:T(8,128)S(1)}, f32[32,1,8,128]{3,2,1,0:T(8,128)S(1)}, u32[]{:S(2)}, u32[]{:S(2)}) collective-permute-start(f32[32,1,8,128]{3,2,1,0:T(8,128)S(1)} %get-tuple-element.20), channel_id=1, source_target_pairs={{0,4},{4,8},{8,12},{12,16},{16,20},{20,24},{24,28},{1,5},{5,9},{9,... | collective-permute-start | bytes 393224 | tf_op jit(solution)/shard_map/ppermute | solution.py:21
  111.7 97.0 %copy-start = (f32[96,8,8,128]{3,2,1,0:T(8,128)S(1)}, f32[96,8,8,128]{3,2,1,0:T(8,128)}, u32[]{:S(2)}) copy-start(f32[96,8,8,128]{3,2,1,0:T(8,128)} %param.5) | copy-start | bytes 9437188
  112.8 1.0 copy-start.2
  115.4 206.9 %reduce-scatter.2.cloned.1.call-start = ((), (), s32[]{:S(2)}) async-start(), calls=%async_computation.2 | async-start | bytes 5242880 | tf_op jit(solution)/shard_map/reduce_scatter | solution.py:87
  248.5 73.8 %copy-start.3 = (f32[32,8,8,128]{3,2,1,0:T(8,128)S(1)}, f32[32,8,8,128]{3,2,1,0:T(8,128)}, u32[]{:S(2)}) copy-start(f32[32,8,8,128]{3,2,1,0:T(8,128)} %copy-done.2) | copy-start | bytes 3145732
  248.6 158.1 %all-gather.5.cloned.1.call-start = ((), (), s32[]{:S(2)}) async-start(), calls=%async_computation.3 | async-start | bytes 5242880 | tf_op jit(solution)/shard_map/all_gather | solution.py:98
  325.2 140.9 %all-reduce.10.cloned.1.call-start = ((), (), s32[]{:S(2)}) async-start(), calls=%async_computation.4 | async-start | bytes 131072 | tf_op jit(solution)/shard_map/psum | solution.py:99
Sparse Core Ops, SparseCore 0:
  115.5 93.1 all-gather.2
  248.7 73.6 reduce-scatter.1
  325.3 81.2 all-gather.4
  414.4 51.6 all-reduce.9
where the time goes:
time: 510 us; the launch traced here: 503 us
  waiting for transfers between devices  306 us (60%)
  other arithmetic  69.2 us (14%)
  starting transfers between devices  56.4 us (11%)
  matrix products  27.3 us (5%)
  blocking collectives  24.3 us (5%)
  between operations  13.9 us (3%)
  local copies, waits for them, and re-layouts  5.53 us (1%)
    all_gather x1, waiting for transfers between devices, per_device(): gathered = lax.all_gather(flat, 'blk', axis=0, tiled=True)  93.3 us
    all_gather x1, waiting for transfers between devices, per_device(): deflated = lax.all_gather(own_deflated, 'blk', axis=0, tiled=True)  81.2 us
    reduce_scatter x1, waiting for transfers between devices, per_device(): lax.psum_scatter(jnp.dot(correlations.T, modes_flat, precision=lax.Precis...  73.7 us
    psum x1, waiting for transfers between devices, per_device(): lax.psum(jnp.dot(deflated, deflated.T, precision=lax.Precision.HIGHEST, p...  51.8 us
    ppermute x8, starting transfers between devices, padded_2(): lax.ppermute(tail, axis, [(i, (i + 1) % count) for i in range(ends)])  45.8 us
    psum x1, blocking collectives, per_device(): lax.psum(jnp.dot(modes_flat, gathered.T, precision=lax.Precision.HIGHEST,...  24.3 us
    concatenate x8, other arithmetic, padded_2(): jnp.concatenate([lax.ppermute(tail, axis, [(i, (i + 1) % count) for i in...  18 us
    another operation x3, other arithmetic, lower_inverse(): lower_factor = jnp.linalg.cholesky(gram)  12.4 us
  transfers between devices with their start and end apart: 20, of which 12 were waited for; matrix products, arithmetic and copies ran while one was open for 0% of the time, Pallas kernels for 0%

commit v1 on v0

--- a/solution.py
+++ b/solution.py
@@ -96,14 +96,17 @@
         tiled=True,
     )
     deflated = lax.all_gather(own_deflated, "blk", axis=0, tiled=True)
-    gram = lax.psum(
-        jnp.dot(
-            deflated,
-            deflated.T,
-            precision=lax.Precision.HIGHEST,
-            preferred_element_type=jnp.float32,
+    gram = jnp.sum(
+        lax.all_gather(
+            jnp.dot(
+                deflated,
+                deflated.T,
+                precision=lax.Precision.HIGHEST,
+                preferred_element_type=jnp.float32,
+            ),
+            "slab",
         ),
-        "slab",
+        axis=0,
     )
     inverse = lower_inverse(gram)
     own_rows = lax.dynamic_slice_in_dim(inverse, lax.axis_index("blk") * own_count, own_count, 0)

time: 510 us -> 465 us (0.912)
  waiting for transfers between devices: 306 us -> 254 us
  blocking collectives: 24.3 us -> 34.1 us
    psum x1 -> x0, waiting for transfers between devices: 51.8 us -> none  [per_device(): lax.psum(jnp.dot(deflated, deflated.T, precision=lax.Precision.HIGHEST, p...]
    all_gather x0 -> x1, blocking collectives: none -> 9.81 us  [per_device(): lax.all_gather(jnp.dot(deflated, deflated.T, precision=lax.Precision.HIGH...]
  transfers between devices with their start and end apart: 20 -> 19, of which waited for: 12 -> 11; matrix products, arithmetic and copies ran while one was open for 0% -> 0% of each run, Pallas kernels for 0% -> 0%
where the time goes in v1:
time: 465 us; the launch traced here: 458 us
  waiting for transfers between devices  254 us (55%)
  other arithmetic  68.4 us (15%)
  starting transfers between devices  56.4 us (12%)
  blocking collectives  34.1 us (7%)
  matrix products  26.7 us (6%)
  between operations  13.9 us (3%)
  local copies, waits for them, and re-layouts  4.67 us (1%)
    all_gather x1, waiting for transfers between devices, per_device(): gathered = lax.all_gather(flat, 'blk', axis=0, tiled=True)  93.3 us
    all_gather x1, waiting for transfers between devices, per_device(): deflated = lax.all_gather(own_deflated, 'blk', axis=0, tiled=True)  81.4 us
    reduce_scatter x1, waiting for transfers between devices, per_device(): lax.psum_scatter(jnp.dot(correlations.T, modes_flat, precision=lax.Precis...  73.6 us
    ppermute x8, starting transfers between devices, padded_2(): lax.ppermute(tail, axis, [(i, (i + 1) % count) for i in range(ends)])  45.8 us
    psum x1, blocking collectives, per_device(): lax.psum(jnp.dot(modes_flat, gathered.T, precision=lax.Precision.HIGHEST,...  24.3 us
    concatenate x8, other arithmetic, padded_2(): jnp.concatenate([lax.ppermute(tail, axis, [(i, (i + 1) % count) for i in...  18 us
    another operation x3, other arithmetic, lower_inverse(): lower_factor = jnp.linalg.cholesky(gram)  12.4 us
    another operation x2, other arithmetic, lower_inverse(): return jax.scipy.linalg.solve_triangular(lower_factor, identity, lower=True)  10.5 us
  transfers between devices with their start and end apart: 19, of which 11 were waited for; matrix products, arithmetic and copies ran while one was open for 0% of the time, Pallas kernels for 0%

profile of v1, /device:TPU:0, one launch (start us, length us, event | category | flops | bytes accessed | tf_op | source)
XLA Modules:
  0.0 458.5 jit_solution(6563126949798105353)
XLA Ops:
  10.8 3.0 collective-permute-start
  14.8 2.2 select_maximum_fusion.14
  21.6 6.1 %collective-permute-start.2 = (f32[32,1,8,128]{3,2,1,0:T(8,128)S(1)}, f32[32,1,8,128]{3,2,1,0:T(8,128)S(1)}, u32[]{:S(2)}, u32[]{:S(2)}) collective-permute-start(f32[32,1,8,128]{3,2,1,0:T(8,128)S(1)} %get-tuple-element.32), channel_id=1, source_target_pairs={{0,4},{4,8},{8,12},{12,16},{16,20},{20,24},{24,28},{1,5},{5,9},{9,... | collective-permute-start | bytes 393224 | tf_op jit(solution)/shard_map/ppermute | solution.py:21
  28.7 2.2 select_maximum_fusion.12
  34.9 6.1 %collective-permute-start.4 = (f32[32,1,8,128]{3,2,1,0:T(8,128)S(1)}, f32[32,1,8,128]{3,2,1,0:T(8,128)S(1)}, u32[]{:S(2)}, u32[]{:S(2)}) collective-permute-start(f32[32,1,8,128]{3,2,1,0:T(8,128)S(1)} %get-tuple-element.30), channel_id=1, source_target_pairs={{0,4},{4,8},{8,12},{12,16},{16,20},{20,24},{24,28},{1,5},{5,9},{9,... | collective-permute-start | bytes 393224 | tf_op jit(solution)/shard_map/ppermute | solution.py:21
  41.8 2.2 select_maximum_fusion.10
  48.1 5.9 %collective-permute-start.6 = (f32[32,1,8,128]{3,2,1,0:T(8,128)S(1)}, f32[32,1,8,128]{3,2,1,0:T(8,128)S(1)}, u32[]{:S(2)}, u32[]{:S(2)}) collective-permute-start(f32[32,1,8,128]{3,2,1,0:T(8,128)S(1)} %get-tuple-element.28), channel_id=1, source_target_pairs={{0,4},{4,8},{8,12},{12,16},{16,20},{20,24},{24,28},{1,5},{5,9},{9,... | collective-permute-start | bytes 393224 | tf_op jit(solution)/shard_map/ppermute | solution.py:21
  61.3 5.9 %collective-permute-start.8 = (f32[32,1,8,128]{3,2,1,0:T(8,128)S(1)}, f32[32,1,8,128]{3,2,1,0:T(8,128)S(1)}, u32[]{:S(2)}, u32[]{:S(2)}) collective-permute-start(f32[32,1,8,128]{3,2,1,0:T(8,128)S(1)} %get-tuple-element.26), channel_id=1, source_target_pairs={{0,4},{4,8},{8,12},{12,16},{16,20},{20,24},{24,28},{1,5},{5,9},{9,... | collective-permute-start | bytes 393224 | tf_op jit(solution)/shard_map/ppermute | solution.py:21
  74.4 6.2 %collective-permute-start.10 = (f32[32,1,8,128]{3,2,1,0:T(8,128)S(1)}, f32[32,1,8,128]{3,2,1,0:T(8,128)S(1)}, u32[]{:S(2)}, u32[]{:S(2)}) collective-permute-start(f32[32,1,8,128]{3,2,1,0:T(8,128)S(1)} %get-tuple-element.24), channel_id=1, source_target_pairs={{0,4},{4,8},{8,12},{12,16},{16,20},{20,24},{24,28},{1,5},{5,9},{9,... | collective-permute-start | bytes 393224 | tf_op jit(solution)/shard_map/ppermute | solution.py:21
  87.6 5.9 %collective-permute-start.12 = (f32[32,1,8,128]{3,2,1,0:T(8,128)S(1)}, f32[32,1,8,128]{3,2,1,0:T(8,128)S(1)}, u32[]{:S(2)}, u32[]{:S(2)}) collective-permute-start(f32[32,1,8,128]{3,2,1,0:T(8,128)S(1)} %get-tuple-element.22), channel_id=1, source_target_pairs={{0,4},{4,8},{8,12},{12,16},{16,20},{20,24},{24,28},{1,5},{5,9},{9,... | collective-permute-start | bytes 393224 | tf_op jit(solution)/shard_map/ppermute | solution.py:21
  94.5 2.2 select_maximum_fusion.2
  100.7 6.6 %collective-permute-start.14 = (f32[32,1,8,128]{3,2,1,0:T(8,128)S(1)}, f32[32,1,8,128]{3,2,1,0:T(8,128)S(1)}, u32[]{:S(2)}, u32[]{:S(2)}) collective-permute-start(f32[32,1,8,128]{3,2,1,0:T(8,128)S(1)} %get-tuple-element.20), channel_id=1, source_target_pairs={{0,4},{4,8},{8,12},{12,16},{16,20},{20,24},{24,28},{1,5},{5,9},{9,... | collective-permute-start | bytes 393224 | tf_op jit(solution)/shard_map/ppermute | solution.py:21
  115.4 93.3 %all-gather.4.cloned.1.call-done = f32[128,8192]{1,0:T(8,128)} async-done(((f32[32,8192]{1,0:T(8,128)}), f32[128,8192]{1,0:T(8,128)}) %all-gather.4.cloned.1.call-update) | async-done | bytes 4194320 | tf_op jit(solution)/shard_map/all_gather | solution.py:77
  208.7 7.6 %fusion.26 = f32[96,128]{0,1:T(8,128)S(1)} fusion(f32[128,8192]{1,0:T(8,128)} %all-gather.4.cloned.1.call-done, f32[12,8,64,128]{3,2,1,0:T(8,128)S(1)} %bitcast.37), kind=kOutput, calls=%fused_computation.95 | convolution fusion | flops 1207959552 | bytes 7389184 | tf_op jit(solution)/shard_map/dot_general | solution.py:79
  216.3 24.3 %psum.7 = f32[96,128]{0,1:T(8,128)S(1)} all-reduce(f32[96,128]{0,1:T(8,128)S(1)} %fusion.26), channel_id=1, replica_groups=mesh['slab'=8,'blk'=4] {'slab'}, use_global_device_ids=true, to_apply=%region_0.1 | all-reduce | flops 12288 | bytes 98304 | tf_op jit(solution)/shard_map/psum | solution.py:78
  240.6 7.8 %fusion.11 = f32[128,8192]{1,0:T(8,128)} fusion(f32[96,128]{0,1:T(8,128)S(1)} %psum.7, f32[12,8,64,128]{3,2,1,0:T(8,128)S(1)} %bitcast.38), kind=kOutput, calls=%fused_computation.56 | convolution fusion | flops 1207959552 | bytes 7389184 | tf_op jit(solution)/shard_map/dot_general | solution.py:88
  248.7 73.6 %reduce-scatter.2.cloned.1.call-done = f32[32,8192]{1,0:T(8,128)} async-done(((f32[128,8192]{1,0:T(8,128)}), f32[32,8192]{1,0:T(8,128)}) %reduce-scatter.2.cloned.1.call-update) | async-done | bytes 1048592 | tf_op jit(solution)/shard_map/reduce_scatter | solution.py:87
  322.3 2.8 fusion.147
  325.2 81.4 %all-gather.6.cloned.1.call-done = f32[128,8192]{1,0:T(8,128)} async-done(((f32[32,8192]{1,0:T(8,128)}), f32[128,8192]{1,0:T(8,128)}) %all-gather.6.cloned.1.call-update) | async-done | bytes 4194320 | tf_op jit(solution)/shard_map/all_gather | solution.py:98
  406.6 7.0 %fusion.163 = f32[128,128]{1,0:T(8,128)S(1)} fusion(f32[128,8192]{1,0:T(8,128)} %all-gather.6.cloned.1.call-done), kind=kOutput, calls=%fused_computation.283 | convolution fusion | flops 1610612736 | bytes 4259840 | tf_op jit(solution)/shard_map/dot_general | solution.py:101
  413.5 9.8 %all-gather = f32[1024,128]{1,0:T(8,128)S(1)} all-gather(f32[128,128]{1,0:T(8,128)S(1)} %fusion.163), channel_id=2, replica_groups=mesh['slab'=8,'blk'=4] {'slab'}, dimensions={0}, use_global_device_ids=true | all-gather | bytes 589824 | tf_op jit(solution)/shard_map/all_gather | solution.py:100
  423.5 11.7 %cholesky.17 = f32[128,128]{1,0:T(8,128)S(1)} custom-call(f32[128,128]{1,0:T(8,128)S(1)} %fusion.142), custom_call_target="Cholesky" | custom-call | tf_op jit(solution)/shard_map/jit(cholesky)/cholesky | solution.py:50
  436.5 9.8 %custom-call.7 = f32[1,128,128]{1,2,0:T(8,128)S(1)} custom-call(f32[1,128,128]{2,1,0:T(8,128)S(1)} %fusion.139), custom_call_target="InvertDiagBlocksLowerTriangular" | custom-call | tf_op jit(solution)/shard_map/jit(_solve_triangular)/triangular_solve | solution.py:52
  446.6 4.0 fusion.25
  (88 shorter events, 56.7 us)
Async XLA Ops:
  6.5 202.1 %all-gather.4.cloned.1.call-start = ((), (), s32[]{:S(2)}) async-start(), calls=%async_computation.1 | async-start | bytes 5242880 | tf_op jit(solution)/shard_map/all_gather | solution.py:77
  9.5 5.1 %collective-permute-start.1 = (f32[32,1,8,128]{3,2,1,0:T(8,128)S(1)}, f32[32,1,8,128]{3,2,1,0:T(8,128)S(1)}, u32[]{:S(2)}, u32[]{:S(2)}) collective-permute-start(f32[32,1,8,128]{3,2,1,0:T(8,128)S(1)} %get-tuple-element.33), channel_id=1, source_target_pairs={{4,0},{8,4},{12,8},{16,12},{20,16},{24,20},{28,24},{5,1},{9,5},{13... | collective-permute-start | bytes 393224 | tf_op jit(solution)/shard_map/ppermute | solution.py:23
  10.8 4.0 collective-permute-start
  18.0 1.2 copy-start.1
  20.3 7.4 %collective-permute-start.3 = (f32[32,1,8,128]{3,2,1,0:T(8,128)S(1)}, f32[32,1,8,128]{3,2,1,0:T(8,128)S(1)}, u32[]{:S(2)}, u32[]{:S(2)}) collective-permute-start(f32[32,1,8,128]{3,2,1,0:T(8,128)S(1)} %get-tuple-element.31), channel_id=1, source_target_pairs={{4,0},{8,4},{12,8},{16,12},{20,16},{24,20},{28,24},{5,1},{9,5},{13... | collective-permute-start | bytes 393224 | tf_op jit(solution)/shard_map/ppermute | solution.py:23
  21.6 7.1 %collective-permute-start.2 = (f32[32,1,8,128]{3,2,1,0:T(8,128)S(1)}, f32[32,1,8,128]{3,2,1,0:T(8,128)S(1)}, u32[]{:S(2)}, u32[]{:S(2)}) collective-permute-start(f32[32,1,8,128]{3,2,1,0:T(8,128)S(1)} %get-tuple-element.32), channel_id=1, source_target_pairs={{0,4},{4,8},{8,12},{12,16},{16,20},{20,24},{24,28},{1,5},{5,9},{9,... | collective-permute-start | bytes 393224 | tf_op jit(solution)/shard_map/ppermute | solution.py:21
  33.6 7.4 %collective-permute-start.5 = (f32[32,1,8,128]{3,2,1,0:T(8,128)S(1)}, f32[32,1,8,128]{3,2,1,0:T(8,128)S(1)}, u32[]{:S(2)}, u32[]{:S(2)}) collective-permute-start(f32[32,1,8,128]{3,2,1,0:T(8,128)S(1)} %get-tuple-element.29), channel_id=1, source_target_pairs={{4,0},{8,4},{12,8},{16,12},{20,16},{24,20},{28,24},{5,1},{9,5},{13... | collective-permute-start | bytes 393224 | tf_op jit(solution)/shard_map/ppermute | solution.py:23
  34.9 6.9 %collective-permute-start.4 = (f32[32,1,8,128]{3,2,1,0:T(8,128)S(1)}, f32[32,1,8,128]{3,2,1,0:T(8,128)S(1)}, u32[]{:S(2)}, u32[]{:S(2)}) collective-permute-start(f32[32,1,8,128]{3,2,1,0:T(8,128)S(1)} %get-tuple-element.30), channel_id=1, source_target_pairs={{0,4},{4,8},{8,12},{12,16},{16,20},{20,24},{24,28},{1,5},{5,9},{9,... | collective-permute-start | bytes 393224 | tf_op jit(solution)/shard_map/ppermute | solution.py:21
  46.8 7.3 %collective-permute-start.7 = (f32[32,1,8,128]{3,2,1,0:T(8,128)S(1)}, f32[32,1,8,128]{3,2,1,0:T(8,128)S(1)}, u32[]{:S(2)}, u32[]{:S(2)}) collective-permute-start(f32[32,1,8,128]{3,2,1,0:T(8,128)S(1)} %get-tuple-element.27), channel_id=1, source_target_pairs={{4,0},{8,4},{12,8},{16,12},{20,16},{24,20},{28,24},{5,1},{9,5},{13... | collective-permute-start | bytes 393224 | tf_op jit(solution)/shard_map/ppermute | solution.py:23
  48.1 6.9 %collective-permute-start.6 = (f32[32,1,8,128]{3,2,1,0:T(8,128)S(1)}, f32[32,1,8,128]{3,2,1,0:T(8,128)S(1)}, u32[]{:S(2)}, u32[]{:S(2)}) collective-permute-start(f32[32,1,8,128]{3,2,1,0:T(8,128)S(1)} %get-tuple-element.28), channel_id=1, source_target_pairs={{0,4},{4,8},{8,12},{12,16},{16,20},{20,24},{24,28},{1,5},{5,9},{9,... | collective-permute-start | bytes 393224 | tf_op jit(solution)/shard_map/ppermute | solution.py:21
  60.0 7.3 %collective-permute-start.9 = (f32[32,1,8,128]{3,2,1,0:T(8,128)S(1)}, f32[32,1,8,128]{3,2,1,0:T(8,128)S(1)}, u32[]{:S(2)}, u32[]{:S(2)}) collective-permute-start(f32[32,1,8,128]{3,2,1,0:T(8,128)S(1)} %get-tuple-element.25), channel_id=1, source_target_pairs={{4,0},{8,4},{12,8},{16,12},{20,16},{24,20},{28,24},{5,1},{9,5},{13... | collective-permute-start | bytes 393224 | tf_op jit(solution)/shard_map/ppermute | solution.py:23
  61.3 6.9 %collective-permute-start.8 = (f32[32,1,8,128]{3,2,1,0:T(8,128)S(1)}, f32[32,1,8,128]{3,2,1,0:T(8,128)S(1)}, u32[]{:S(2)}, u32[]{:S(2)}) collective-permute-start(f32[32,1,8,128]{3,2,1,0:T(8,128)S(1)} %get-tuple-element.26), channel_id=1, source_target_pairs={{0,4},{4,8},{8,12},{12,16},{16,20},{20,24},{24,28},{1,5},{5,9},{9,... | collective-permute-start | bytes 393224 | tf_op jit(solution)/shard_map/ppermute | solution.py:21
  73.1 7.5 %collective-permute-start.11 = (f32[32,1,8,128]{3,2,1,0:T(8,128)S(1)}, f32[32,1,8,128]{3,2,1,0:T(8,128)S(1)}, u32[]{:S(2)}, u32[]{:S(2)}) collective-permute-start(f32[32,1,8,128]{3,2,1,0:T(8,128)S(1)} %get-tuple-element.23), channel_id=1, source_target_pairs={{4,0},{8,4},{12,8},{16,12},{20,16},{24,20},{28,24},{5,1},{9,5},{13... | collective-permute-start | bytes 393224 | tf_op jit(solution)/shard_map/ppermute | solution.py:23
  74.4 6.9 %collective-permute-start.10 = (f32[32,1,8,128]{3,2,1,0:T(8,128)S(1)}, f32[32,1,8,128]{3,2,1,0:T(8,128)S(1)}, u32[]{:S(2)}, u32[]{:S(2)}) collective-permute-start(f32[32,1,8,128]{3,2,1,0:T(8,128)S(1)} %get-tuple-element.24), channel_id=1, source_target_pairs={{0,4},{4,8},{8,12},{12,16},{16,20},{20,24},{24,28},{1,5},{5,9},{9,... | collective-permute-start | bytes 393224 | tf_op jit(solution)/shard_map/ppermute | solution.py:21
  86.3 7.3 %collective-permute-start.13 = (f32[32,1,8,128]{3,2,1,0:T(8,128)S(1)}, f32[32,1,8,128]{3,2,1,0:T(8,128)S(1)}, u32[]{:S(2)}, u32[]{:S(2)}) collective-permute-start(f32[32,1,8,128]{3,2,1,0:T(8,128)S(1)} %get-tuple-element.21), channel_id=1, source_target_pairs={{4,0},{8,4},{12,8},{16,12},{20,16},{24,20},{28,24},{5,1},{9,5},{13... | collective-permute-start | bytes 393224 | tf_op jit(solution)/shard_map/ppermute | solution.py:23
  87.6 6.9 %collective-permute-start.12 = (f32[32,1,8,128]{3,2,1,0:T(8,128)S(1)}, f32[32,1,8,128]{3,2,1,0:T(8,128)S(1)}, u32[]{:S(2)}, u32[]{:S(2)}) collective-permute-start(f32[32,1,8,128]{3,2,1,0:T(8,128)S(1)} %get-tuple-element.22), channel_id=1, source_target_pairs={{0,4},{4,8},{8,12},{12,16},{16,20},{20,24},{24,28},{1,5},{5,9},{9,... | collective-permute-start | bytes 393224 | tf_op jit(solution)/shard_map/ppermute | solution.py:21
  99.4 7.9 %collective-permute-start.15 = (f32[32,1,8,128]{3,2,1,0:T(8,128)S(1)}, f32[32,1,8,128]{3,2,1,0:T(8,128)S(1)}, u32[]{:S(2)}, u32[]{:S(2)}) collective-permute-start(f32[32,1,8,128]{3,2,1,0:T(8,128)S(1)} %get-tuple-element.19), channel_id=1, source_target_pairs={{4,0},{8,4},{12,8},{16,12},{20,16},{24,20},{28,24},{5,1},{9,5},{13... | collective-permute-start | bytes 393224 | tf_op jit(solution)/shard_map/ppermute | solution.py:23
  100.7 7.1 %collective-permute-start.14 = (f32[32,1,8,128]{3,2,1,0:T(8,128)S(1)}, f32[32,1,8,128]{3,2,1,0:T(8,128)S(1)}, u32[]{:S(2)}, u32[]{:S(2)}) collective-permute-start(f32[32,1,8,128]{3,2,1,0:T(8,128)S(1)} %get-tuple-element.20), channel_id=1, source_target_pairs={{0,4},{4,8},{8,12},{12,16},{16,20},{20,24},{24,28},{1,5},{5,9},{9,... | collective-permute-start | bytes 393224 | tf_op jit(solution)/shard_map/ppermute | solution.py:21
  111.7 97.0 %copy-start = (f32[96,8,8,128]{3,2,1,0:T(8,128)S(1)}, f32[96,8,8,128]{3,2,1,0:T(8,128)}, u32[]{:S(2)}) copy-start(f32[96,8,8,128]{3,2,1,0:T(8,128)} %param.5) | copy-start | bytes 9437188
  112.8 1.0 copy-start.2
  115.4 206.9 %reduce-scatter.2.cloned.1.call-start = ((), (), s32[]{:S(2)}) async-start(), calls=%async_computation.2 | async-start | bytes 5242880 | tf_op jit(solution)/shard_map/reduce_scatter | solution.py:87
  248.5 73.8 %copy-start.3 = (f32[32,8,8,128]{3,2,1,0:T(8,128)S(1)}, f32[32,8,8,128]{3,2,1,0:T(8,128)}, u32[]{:S(2)}) copy-start(f32[32,8,8,128]{3,2,1,0:T(8,128)} %copy-done.2) | copy-start | bytes 3145732
  248.5 158.1 %all-gather.6.cloned.1.call-start = ((), (), s32[]{:S(2)}) async-start(), calls=%async_computation.3 | async-start | bytes 5242880 | tf_op jit(solution)/shard_map/all_gather | solution.py:98
Sparse Core Ops, SparseCore 0:
  115.5 93.1 all-gather.3
  248.6 73.6 reduce-scatter.1
  325.3 81.2 all-gather.5
